TPU v7x, 32 devices: a whole 2x2x4 slice. The times are simulated.
32 devices in a mesh: vol: 16 (over z, x, core), slab: 2 (over y).
Axes of the slice: x: 2, y: 2, z: 4, core: 2. Of those that a mesh axis runs over, the one named last changes fastest.
Arguments:
- volumes: bfloat16 [32, 4, 16, 16, 64], P('vol', None, 'slab'), may hold values from -6 to 6
- w_first: bfloat16 [32, 108], replicated, may hold values from -0.625 to 0.625
- w_second: bfloat16 [64, 864], replicated, may hold values from -0.21875 to 0.21875
- w_third: bfloat16 [128, 1728], replicated, may hold values from -0.15625 to 0.15625
- map_grad: bfloat16 [32, 128, 4, 4, 16], P(('vol', 'slab')), may hold values from -6 to 6
Outputs:
- grad_first: float32 [32, 108], replicated
- grad_second: float32 [64, 864], replicated
- grad_third: float32 [128, 1728], replicated
All inputs are finite; a program needn't handle non-finite values.
Results may differ from a plain program's by a relative error of at most 0.0071.
Values may be sent and summed in bfloat16 or wider, within the bound.
A program may use at most 64 MiB of HBM per device.

v0:
```python
import functools

import jax
import jax.numpy as jnp
import numpy as np
from jax import lax
from jax.experimental import pallas as pl
from jax.experimental.pallas import tpu as pltpu
from jax.sharding import PartitionSpec as P

MESH = pl.DeviceIdType.MESH
BLOCK = 8


def one_hot(rows, cols, pairs):
    table = np.zeros((rows, cols), np.float32)
    for row, col in pairs:
        table[row, col] = 1.0
    return table


def cell_picks(depth, height, stride):
    out_depth, out_height = depth // stride, height // stride
    pairs = []
    for a in range(3):
        for b in range(3):
            for i in range(out_depth):
                for j in range(out_height):
                    z, y = stride * i + a - 1, stride * j + b - 1
                    if 0 <= z < depth and 0 <= y < height:
                        row = ((a * 3 + b) * out_depth + i) * out_height + j
                        pairs.append((row, z * height + y))
    return one_hot(9 * out_depth * out_height, depth * height, pairs)


def tables_of(channels, depth, height, width):
    blocks = width // (2 * BLOCK)
    spread = np.zeros((channels, width, blocks * 128), np.float32)
    for block in range(blocks):
        for at in range(2 * BLOCK + 1):
            x = 2 * BLOCK * block - 1 + at
            if x >= 0:
                for k in range(channels):
                    spread[k, x, block * 128 + at * channels + k] = 1.0
    taps = one_hot(
        27 * channels,
        9 * 128,
        [
            (pair * 3 * channels + lane, pair * 128 + lane)
            for pair in range(9)
            for lane in range(3 * channels)
        ],
    )
    plane, length = (depth // 4) * (height // 4), width // 4
    order = one_hot(
        plane * length,
        plane * length,
        [(l * plane + p, p * length + l) for l in range(length) for p in range(plane)],
    )
    second = cell_picks(depth // 2, height // 2, 2)
    third = cell_picks(depth // 4, height // 4, 1)
    tables = (spread, cell_picks(depth, height, 2), second, third, second.T, third.T, taps, order)
    return [jnp.asarray(table, jnp.bfloat16) for table in tables]


def contract(lhs, rhs, rhs_dim=0):
    return lax.dot_general(
        lhs, rhs, (((1,), (rhs_dim,)), ((), ())), preferred_element_type=jnp.float32
    )


def contract_fine(lhs, rhs):
    coarse = half(rhs)
    return contract(lhs, coarse) + contract(lhs, half(rhs - coarse.astype(jnp.float32)))


def sigmoid(pre):
    return 1.0 / (1.0 + jnp.exp(-pre))


def slope_of(pre):
    sigma = sigmoid(pre)
    return sigma * (1.0 + pre * (1.0 - sigma))


def half(value):
    return value.astype(jnp.bfloat16)


def sample_kernel(shapes, vol, w1, w2, w3, mg, spread, pick1, pick2, pick3, back2, back3, taps,
                  order, out, p1, p2, p3, w1b, w2p, w3p, a2, even3, odd3, even2, odd2, rows2, g2, g3):
    f32 = jnp.float32
    channels = vol.shape[0]
    c1, c2, c3 = w1.shape[0], w2.shape[0], w3.shape[0]
    blocks = spread.shape[2] // 128
    plane1, plane2 = pick1.shape[0] // 9, pick2.shape[0] // 9
    length2 = mg.shape[1] // plane2
    width1 = blocks * BLOCK * c1
    width2 = length2 * c2

    placed = contract(vol[0], spread[0])
    for k in range(1, channels):
        placed = placed + contract(vol[k], spread[k])
    r1 = half(contract(pick1[...], half(placed)))
    for pair in range(9):
        for block in range(blocks):
            p1[block * plane1 : (block + 1) * plane1, pair * 128 : (pair + 1) * 128] = r1[
                pair * plane1 : (pair + 1) * plane1, block * 128 : (block + 1) * 128
            ]
    wide = contract(w1[...], taps[...])
    for pair in range(9):
        tile = wide[:, pair * 128 : (pair + 1) * 128]
        for l in range(BLOCK):
            moved = pltpu.roll(tile, 2 * l * channels, 1) if l else tile
            w1b[l * c1 : (l + 1) * c1, pair * 128 : (pair + 1) * 128] = half(moved)
    w2p[...] = jnp.zeros_like(w2p)
    w3p[...] = jnp.zeros_like(w3p)
    for pair in range(9):
        w2p[:, pair * 128 : pair * 128 + 3 * c1] = w2[:, pair * 3 * c1 : (pair + 1) * 3 * c1]
        w3p[:, pair * 256 : pair * 256 + 3 * c2] = w3[:, pair * 3 * c2 : (pair + 1) * 3 * c2]

    pre1 = contract(p1[...], w1b[...], 1)
    act1 = half(pre1 * sigmoid(pre1))
    a1 = jnp.concatenate(
        [act1[block * plane1 : (block + 1) * plane1, :] for block in range(blocks)], axis=1
    )
    r2 = contract(pick2[...], a1)
    r2 = jnp.concatenate([r2, jnp.zeros((9 * plane2, 128), f32)], axis=1)
    sides = (half(pltpu.roll(r2, c1, 1)), half(pltpu.roll(r2, width1 + 128 - c1, 1)))
    for l in range(length2):
        chunk = sides[l % 2][:, (l // 2) * 128 : (l // 2 + 1) * 128]
        for pair in range(9):
            p2[l * plane2 : (l + 1) * plane2, pair * 128 : (pair + 1) * 128] = chunk[
                pair * plane2 : (pair + 1) * plane2, :
            ]
    pre2 = contract(p2[...], w2p[...], 1)
    act2 = pre2 * sigmoid(pre2)
    for l in range(length2):
        a2[:, l * c2 : (l + 1) * c2] = act2[l * plane2 : (l + 1) * plane2, :]
    r3 = contract(pick3[...], half(a2[...]))
    r3 = jnp.concatenate([r3, jnp.zeros((9 * plane2, 256), f32)], axis=1)
    sides = (half(pltpu.roll(r3, c2, 1)), half(r3))
    for l in range(length2):
        chunk = sides[l % 2][:, (l // 2) * 128 : (l // 2) * 128 + 256]
        for pair in range(9):
            p3[l * plane2 : (l + 1) * plane2, pair * 256 : (pair + 1) * 256] = chunk[
                pair * plane2 : (pair + 1) * plane2, :
            ]
    pre3 = contract(p3[...], w3p[...], 1)
    given = contract(order[...], mg[...], 1)
    slope3 = given * slope_of(pre3)
    delta3 = half(slope3)
    grad3 = contract(half(slope3.T), p3[...])
    g3[...] = jnp.zeros_like(g3)
    for pair in range(9):
        g3[:, pair * 3 * c2 : (pair + 1) * 3 * c2] = grad3[:, pair * 256 : pair * 256 + 3 * c2]

    spread3 = contract(delta3, w3p[...])
    for pair in range(9):
        for side, holder in ((0, even3), (1, odd3)):
            for tile in range(length2 // 2 + 1):
                total = None
                for part in range(2):
                    l = 2 * (tile - part) + side
                    if 0 <= l < length2:
                        piece = spread3[
                            l * plane2 : (l + 1) * plane2,
                            pair * 256 + part * 128 : pair * 256 + part * 128 + 128,
                        ]
                        total = piece if total is None else total + piece
                holder[pair * plane2 : (pair + 1) * plane2, tile * 128 : (tile + 1) * 128] = total
    down = contract_fine(back3[...], even3[...])
    down = pltpu.roll(down, down.shape[1] - c2, 1) + contract_fine(back3[...], odd3[...])
    for l in range(length2):
        rows2[l * plane2 : (l + 1) * plane2, :] = down[:, l * c2 : (l + 1) * c2]
    slope2 = half(rows2[...]).astype(f32) * slope_of(pre2)
    delta2 = half(slope2)
    grad2 = contract(half(slope2.T), p2[...])
    g2[...] = jnp.zeros_like(g2)
    for pair in range(9):
        g2[:, pair * 3 * c1 : (pair + 1) * 3 * c1] = grad2[:, pair * 128 : pair * 128 + 3 * c1]

    spread2 = contract(delta2, w2p[...])
    for pair in range(9):
        for l in range(length2):
            holder = odd2 if l % 2 else even2
            holder[pair * plane2 : (pair + 1) * plane2, (l // 2) * 128 : (l // 2 + 1) * 128] = spread2[
                l * plane2 : (l + 1) * plane2, pair * 128 : (pair + 1) * 128
            ]
    tail = jnp.zeros((plane1, 128), f32)
    left = jnp.concatenate([contract_fine(back2[...], even2[...]), tail], axis=1)
    right = jnp.concatenate([contract_fine(back2[...], odd2[...]), tail], axis=1)
    down = pltpu.roll(left, width1 + 128 - c1, 1) + pltpu.roll(right, c1, 1)
    step = BLOCK * c1
    down = jnp.concatenate([down[:, block * step : (block + 1) * step] for block in range(blocks)], axis=0)
    slope1 = down * slope_of(pre1)
    grad1 = contract(half(slope1.T), p1[...])
    tiles = []
    for pair in range(9):
        total = grad1[:c1, pair * 128 : (pair + 1) * 128]
        for l in range(1, BLOCK):
            tile = grad1[l * c1 : (l + 1) * c1, pair * 128 : (pair + 1) * 128]
            total = total + pltpu.roll(tile, 128 - 2 * l * channels, 1)
        tiles.append(half(total))
    first = contract(jnp.concatenate(tiles, axis=1), taps[...], 1)

    out[...] = jnp.zeros_like(out)
    grads = (first, g2, g3)
    for index, base, rows, start, width in tiles_of(shapes):
        if index == 0:
            out[base : base + rows, :width] = half(first)
        else:
            out[base : base + rows, :] = half(grads[index][:, start : start + 128])


def sample_grads(volume, w_first, w_second, w_third, map_grad, shapes, rows):
    channels, depth, height, width = volume.shape
    tables = tables_of(channels, depth, height, width)
    c1, c2, c3 = w_first.shape[0], w_second.shape[0], w_third.shape[0]
    plane1 = depth * height // 4
    plane2 = depth * height // 16
    length2 = width // 4
    cells = plane2 * length2
    bf16, f32 = jnp.bfloat16, jnp.float32
    scratch = [
        ((width // (2 * BLOCK) * plane1, 9 * 128), bf16),
        ((cells, 9 * 128), bf16),
        ((cells, 9 * 256), bf16),
        ((BLOCK * c1, 9 * 128), bf16),
        ((c2, 9 * 128), bf16),
        ((c3, 9 * 256), bf16),
        ((plane2, length2 * c2), f32),
        ((9 * plane2, length2 * c2 + 128), f32),
        ((9 * plane2, length2 * c2 + 128), f32),
        ((9 * plane2, width // 2 * c1), f32),
        ((9 * plane2, width // 2 * c1), f32),
        ((cells, c2), f32),
        ((c2, pl.cdiv(27 * c1, 128) * 128), f32),
        ((c3, pl.cdiv(27 * c2, 128) * 128), f32),
    ]
    operands = (
        volume.reshape(channels, depth * height, width),
        w_first,
        w_second,
        w_third,
        map_grad.reshape(c3, cells),
        *tables,
    )
    return pl.pallas_call(
        functools.partial(sample_kernel, shapes),
        out_shape=jax.ShapeDtypeStruct((rows, 128), bf16),
        in_specs=[pl.BlockSpec(memory_space=pltpu.VMEM)] * len(operands),
        out_specs=pl.BlockSpec(memory_space=pltpu.VMEM),
        scratch_shapes=[pltpu.VMEM(shape, kind) for shape, kind in scratch],
        compiler_params=pltpu.CompilerParams(vmem_limit_bytes=56 << 20),
        name="sample_grads",
    )(*operands)


def packed_rows(shapes):
    return sum(pl.cdiv(cols, 128) * rows for rows, cols in shapes)


def tiles_of(shapes):
    base = 0
    for index, (rows, cols) in enumerate(shapes):
        for start in range(0, cols, 128):
            yield index, base, rows, start, min(128, cols - start)
            base += rows


def piece_rows(shapes, devices):
    return pl.cdiv(pl.cdiv(packed_rows(shapes), devices), 16) * 16


def reduce_kernel(shapes, slabs, chips, piece, factor, x_ref, *refs):
    outs = refs[: len(shapes)]
    from_pair, mine, landed, total, whole = refs[len(shapes) : len(shapes) + 5]
    pair_sems, send_sems, land_sems, back_send, back_land, fwd_send, fwd_land = refs[len(shapes) + 5 :]
    vol = lax.axis_index("vol")
    slab = lax.axis_index("slab")
    core = lax.rem(vol, 2)
    me = (vol // 2) * slabs + slab
    pair = (vol + 1 - 2 * core, slab)
    half = chips * piece

    def peer_of(step):
        other = lax.rem(me + step, chips)
        return ((other // slabs) * 2 + core, lax.rem(other, slabs))

    def rows_of(index):
        return pl.ds(pl.multiple_of(index * piece, 16), piece)

    barrier = pltpu.get_barrier_semaphore()
    pl.semaphore_signal(barrier, inc=1, device_id=pair, device_id_type=MESH)

    def greet(step, carry):
        pl.semaphore_signal(barrier, inc=1, device_id=peer_of(step), device_id_type=MESH)
        return carry

    lax.fori_loop(1, chips, greet, 0)
    pl.semaphore_wait(barrier, chips)

    swap = pltpu.make_async_remote_copy(
        src_ref=x_ref.at[pl.ds(pl.multiple_of((1 - core) * half, 16), half)],
        dst_ref=from_pair,
        send_sem=pair_sems.at[0],
        recv_sem=pair_sems.at[1],
        device_id=pair,
        device_id_type=MESH,
    )
    swap.start()
    swap.wait()
    own = x_ref[pl.ds(pl.multiple_of(core * half, 16), half), :].astype(jnp.float32)
    mine[...] = (own + from_pair[...].astype(jnp.float32)).astype(jnp.bfloat16)

    def scatter(step):
        other = lax.rem(me + step, chips)
        return pltpu.make_async_remote_copy(
            src_ref=mine.at[rows_of(other)],
            dst_ref=landed.at[rows_of(step)],
            send_sem=send_sems.at[step],
            recv_sem=land_sems.at[step],
            device_id=peer_of(step),
            device_id_type=MESH,
        )

    def start_scatter(step, carry):
        scatter(step).start()
        return carry

    lax.fori_loop(1, chips, start_scatter, 0)

    def add_landed(step, running):
        scatter(step).wait_recv()
        return running + landed[rows_of(step), :].astype(jnp.float32)

    summed = lax.fori_loop(1, chips, add_landed, mine[rows_of(me), :].astype(jnp.float32))
    total[...] = summed.astype(jnp.bfloat16)
    base = core * chips
    whole[rows_of(base + me), :] = total[...]

    def spread(step):
        return pltpu.make_async_remote_copy(
            src_ref=total,
            dst_ref=whole.at[rows_of(base + me)],
            send_sem=back_send.at[step],
            recv_sem=back_land.at[step],
            device_id=peer_of(step),
            device_id_type=MESH,
        )

    def start_spread(step, carry):
        spread(step).start()
        return carry

    lax.fori_loop(1, chips, start_spread, 0)

    def forward_on(step):
        index = base + lax.rem(me - step + chips, chips)
        return pltpu.make_async_remote_copy(
            src_ref=whole.at[rows_of(index)],
            dst_ref=whole.at[rows_of(index)],
            send_sem=fwd_send.at[step],
            recv_sem=fwd_land.at[step],
            device_id=pair,
            device_id_type=MESH,
        )

    forward_on(0).start()

    def hand_on(step, carry):
        spread(step).wait_recv()
        forward_on(step).start()
        return carry

    lax.fori_loop(1, chips, hand_on, 0)

    def settle(step, carry):
        forward_on(step).wait()
        return carry

    lax.fori_loop(0, chips, settle, 0)

    def drain(step, carry):
        scatter(step).wait_send()
        spread(step).wait_send()
        return carry

    lax.fori_loop(1, chips, drain, 0)
    for index, base_row, rows, start, width in tiles_of(shapes):
        tile = whole[base_row : base_row + rows, :].astype(jnp.float32) * factor
        outs[index][:, start : start + width] = tile[:, :width]


def reduce_all(packed, shapes, factor):
    slabs = lax.axis_size("slab")
    devices = lax.axis_size("vol") * slabs
    chips = devices // 2
    piece = piece_rows(shapes, devices)
    dma = pltpu.SemaphoreType.DMA
    return pl.pallas_call(
        functools.partial(reduce_kernel, shapes, slabs, chips, piece, factor),
        out_shape=[jax.ShapeDtypeStruct(shape, jnp.float32) for shape in shapes],
        in_specs=[pl.BlockSpec(memory_space=pltpu.VMEM)],
        out_specs=[pl.BlockSpec(memory_space=pltpu.VMEM)] * len(shapes),
        scratch_shapes=[
            pltpu.VMEM((chips * piece, 128), jnp.bfloat16),
            pltpu.VMEM((chips * piece, 128), jnp.bfloat16),
            pltpu.VMEM((chips * piece, 128), jnp.bfloat16),
            pltpu.VMEM((piece, 128), jnp.bfloat16),
            pltpu.VMEM((devices * piece, 128), jnp.bfloat16),
            dma((2,)),
            dma((chips,)),
            dma((chips,)),
            dma((chips,)),
            dma((chips,)),
            dma((chips,)),
            dma((chips,)),
        ],
        compiler_params=pltpu.CompilerParams(collective_id=0, has_side_effects=True),
        name="reduce_all",
    )(packed)


def per_device(volumes, w_first, w_second, w_third, map_grad):
    volume = lax.all_to_all(volumes, "slab", split_axis=0, concat_axis=2, tiled=True)
    devices = lax.axis_size("vol") * lax.axis_size("slab")
    factor = 1.0 / (map_grad.shape[0] * devices)
    shapes = (w_first.shape, w_second.shape, w_third.shape)
    rows = devices * piece_rows(shapes, devices)
    packed = sample_grads(volume[0], w_first, w_second, w_third, map_grad[0], shapes, rows)
    return tuple(reduce_all(packed, shapes, factor))


def solution(mesh):
    return jax.shard_map(
        per_device,
        mesh=mesh,
        in_specs=(
            P("vol", None, "slab", None, None),
            P(),
            P(),
            P(),
            P(("vol", "slab"), None, None, None, None),
        ),
        out_specs=(P(), P(), P()),
        check_vma=False,
    )
```

profile of v0, /device:TPU:25, one launch (start us, length us, event | category | flops | bytes accessed | tf_op | source)
XLA Modules:
  0.0 51.0 jit_solution(2758565745170450556)
XLA Ops:
  0.6 0.0 copy-start
  0.6 1.9 %reshape.7 = bf16[2,2,16384]{2,1,0:T(2,128)(2,1)} reshape(bf16[2,4,8,16,64]{4,3,2,1,0:T(8,128)(2,1)} %param.13) | data formatting | bytes 262144
  2.5 0.0 copy-start.2
  2.5 3.5 %all-to-all-start = ((bf16[2,2,16384]{2,1,0:T(2,128)(2,1)}), bf16[2,2,16384]{2,1,0:T(2,128)(2,1)S(1)}, u32[]{:S(2)}, u32[]{:S(2)}) async-start(bf16[2,2,16384]{2,1,0:T(2,128)(2,1)} %reshape.7), calls=%async_computation | async-start | bytes 262144 | tf_op jit(solution)/shard_map/all_to_all | solution.py:427
  6.1 0.0 copy-done.2
  6.1 0.7 %copy.22.mg = bf16[128,256]{1,0:T(8,128)(2,1)} copy(bf16[128,256]{0,1:T(8,128)(2,1)S(1)} %bitcast.7) | data formatting | bytes 131072 | tf_op jit(solution)/shard_map/reshape;squeeze | solution.py:246
  6.8 0.0 copy-done
  6.8 1.0 %copy.21.w3 = bf16[128,1728]{1,0:T(8,128)(2,1)} copy(bf16[128,1728]{0,1:T(8,128)(2,1)S(1)} %copy-done) | data formatting | bytes 884736 | tf_op args[3]
  7.8 1.6 %all-to-all-done = bf16[2,2,16384]{2,1,0:T(2,128)(2,1)S(1)} async-done(((bf16[2,2,16384]{2,1,0:T(2,128)(2,1)}), bf16[2,2,16384]{2,1,0:T(2,128)(2,1)S(1)}, u32[]{:S(2)}, u32[]{:S(2)}) %all-to-all-start) | async-done | bytes 131104 | tf_op jit(solution)/shard_map/all_to_all | solution.py:427
  9.4 0.2 reshape.8
  9.6 0.7 %copy.20 = bf16[1,4,2,8,16,64]{5,4,3,2,1,0:T(8,128)(2,1)} copy(bf16[1,4,2,8,16,64]{5,4,3,1,2,0:T(8,128)(2,1)S(1)} %bitcast.6) | data formatting | bytes 262144 | tf_op jit(solution)/shard_map/all_to_all | solution.py:427
  10.3 8.1 %sample_grads.1.x_ref = bf16[2560,128]{1,0:T(8,128)(2,1)} custom-call(bf16[4,256,64]{2,1,0:T(8,128)(2,1)} %bitcast.5, bf16[32,108]{1,0:T(8,128)(2,1)} %w1.1, bf16[64,864]{1,0:T(8,128)(2,1)} %w2.1, bf16[128,1728]{1,0:T(8,128)(2,1)} %copy.21.w3, bf16[128,256]{1,0:T(8,128)(2,1)} %copy.22.mg, bf16[4,64,512]{2,1,0:T(8,128)(2,1)} %constant.16.clone.spread, ...), custom_call_target="tpu_custom_call" | custom-call | tf_op jit(solution)/shard_map/sample_grads/pallas_call | solution.py:249
  18.4 28.9 %reduce_all.1 = (f32[32,108]{1,0:T(8,128)}, f32[64,864]{1,0:T(8,128)}, f32[128,1728]{1,0:T(8,128)}) custom-call(bf16[2560,128]{1,0:T(8,128)(2,1)} %sample_grads.1.x_ref), custom_call_target="tpu_custom_call" | custom-call | tf_op jit(solution)/shard_map/reduce_all/pallas_call | solution.py:402
  47.3 0.0 copy-start.3
  47.3 0.0 copy-start.1
  47.3 2.4 %copy.23 = f32[128,1728]{0,1:T(8,128)} copy(f32[128,1728]{1,0:T(8,128)} %get-tuple-element.8) | data formatting | bytes 1769472 | tf_op jit(solution)/shard_map/reduce_all/pallas_call | solution.py:402
  49.8 0.0 copy-done.3
  49.8 0.6 %copy.26 = f32[32,108]{1,0:T(8,128)} copy(f32[32,108]{1,0:T(8,128)S(1)} %copy-done.3) | data formatting | bytes 27648
  50.4 0.0 copy-done.1
  50.4 0.7 %copy.27 = f32[64,864]{1,0:T(8,128)} copy(f32[64,864]{1,0:T(8,128)S(1)} %copy-done.1) | data formatting | bytes 442368
Async XLA Ops:
  0.6 6.2 %copy-start = (bf16[128,1728]{0,1:T(8,128)(2,1)S(1)}, bf16[128,1728]{0,1:T(8,128)(2,1)}, u32[]{:S(2)}) copy-start(bf16[128,1728]{0,1:T(8,128)(2,1)} %param.16) | copy-start | bytes 1327108
  2.5 3.5 %copy-start.2 = (bf16[1,128,4,4,16]{1,4,3,2,0:T(8,128)(2,1)S(1)}, bf16[1,128,4,4,16]{1,4,3,2,0:T(8,128)(2,1)}, u32[]{:S(2)}) copy-start(bf16[1,128,4,4,16]{1,4,3,2,0:T(8,128)(2,1)} %param.17) | copy-start | bytes 196612
  2.5 6.8 %all-to-all-start = ((bf16[2,2,16384]{2,1,0:T(2,128)(2,1)}), bf16[2,2,16384]{2,1,0:T(2,128)(2,1)S(1)}, u32[]{:S(2)}, u32[]{:S(2)}) async-start(bf16[2,2,16384]{2,1,0:T(2,128)(2,1)} %reshape.7), calls=%async_computation | async-start | bytes 262144 | tf_op jit(solution)/shard_map/all_to_all | solution.py:427
  47.3 2.5 %copy-start.3 = (f32[32,108]{1,0:T(8,128)S(1)}, f32[32,108]{1,0:T(8,128)}, u32[]{:S(2)}) copy-start(f32[32,108]{1,0:T(8,128)} %get-tuple-element.12) | copy-start | bytes 41476
  47.3 3.1 %copy-start.1 = (f32[64,864]{1,0:T(8,128)S(1)}, f32[64,864]{1,0:T(8,128)}, u32[]{:S(2)}) copy-start(f32[64,864]{1,0:T(8,128)} %get-tuple-element.13) | copy-start | bytes 663556
where the time goes:
time: 51.4 us; the launch traced here: 51 us
  Pallas kernels  37 us (72%)
  local copies, waits for them, and re-layouts  8.31 us (16%)
  starting transfers between devices  3.51 us (7%)
  waiting for transfers between devices  1.56 us (3%)
  between operations  0.69 us (1%)
    pallas_call x1, Pallas kernels, reduce_all(): pl.pallas_call(functools.partial(reduce_kernel, shapes, slabs, chips, pie...  28.9 us
    pallas_call x1, Pallas kernels, sample_grads(): pl.pallas_call(functools.partial(sample_kernel, shapes), out_shape=jax.Sh...  8.11 us
    unnamed x13, local copies, waits for them, and re-layouts  4.42 us
    all_to_all x1, starting transfers between devices, per_device(): lax.all_to_all(volumes, 'slab', split_axis=0, concat_axis=2, tiled=True)  3.51 us
    pallas_call x1, local copies, waits for them, and re-layouts, reduce_all(): pl.pallas_call(functools.partial(reduce_kernel, shapes, slabs, chips, pie...  2.43 us
    all_to_all x1, waiting for transfers between devices, per_device(): lax.all_to_all(volumes, 'slab', split_axis=0, concat_axis=2, tiled=True)  1.56 us
  transfers between devices with their start and end apart: 1, of which 1 were waited for; matrix products, arithmetic and copies ran while one was open for 3% of the time, Pallas kernels for 0%

commit v1 on v0

v1 whole, which is shorter than its diff:
```python
import functools

import jax
import jax.numpy as jnp
import numpy as np
from jax import lax
from jax.experimental import pallas as pl
from jax.experimental.pallas import tpu as pltpu
from jax.sharding import PartitionSpec as P

MESH = pl.DeviceIdType.MESH
BLOCK = 8


def one_hot(rows, cols, pairs):
    table = np.zeros((rows, cols), np.float32)
    for row, col in pairs:
        table[row, col] = 1.0
    return table


def cell_picks(depth, height, stride):
    out_depth, out_height = depth // stride, height // stride
    pairs = []
    for a in range(3):
        for b in range(3):
            for i in range(out_depth):
                for j in range(out_height):
                    z, y = stride * i + a - 1, stride * j + b - 1
                    if 0 <= z < depth and 0 <= y < height:
                        row = ((a * 3 + b) * out_depth + i) * out_height + j
                        pairs.append((row, z * height + y))
    return one_hot(9 * out_depth * out_height, depth * height, pairs)


def tables_of(channels, depth, height, width):
    blocks = width // (2 * BLOCK)
    spread = np.zeros((channels, width, blocks * 128), np.float32)
    for block in range(blocks):
        for at in range(2 * BLOCK + 1):
            x = 2 * BLOCK * block - 1 + at
            if x >= 0:
                for k in range(channels):
                    spread[k, x, block * 128 + at * channels + k] = 1.0
    taps = one_hot(
        27 * channels,
        9 * 128,
        [
            (pair * 3 * channels + lane, pair * 128 + lane)
            for pair in range(9)
            for lane in range(3 * channels)
        ],
    )
    plane, length = (depth // 4) * (height // 4), width // 4
    order = one_hot(
        plane * length,
        plane * length,
        [(l * plane + p, p * length + l) for l in range(length) for p in range(plane)],
    )
    second = cell_picks(depth // 2, height // 2, 2)
    third = cell_picks(depth // 4, height // 4, 1)
    tables = (spread, cell_picks(depth, height, 2), second, third, second.T, third.T, taps, order)
    return [jnp.asarray(table, jnp.bfloat16) for table in tables]


def contract(lhs, rhs, rhs_dim=0):
    return lax.dot_general(
        lhs, rhs, (((1,), (rhs_dim,)), ((), ())), preferred_element_type=jnp.float32
    )


def contract_fine(lhs, rhs):
    coarse = half(rhs)
    return contract(lhs, coarse) + contract(lhs, half(rhs - coarse.astype(jnp.float32)))


def sigmoid(pre):
    return 1.0 / (1.0 + jnp.exp(-pre))


def slope_of(pre):
    sigma = sigmoid(pre)
    return sigma * (1.0 + pre * (1.0 - sigma))


def half(value):
    return value.astype(jnp.bfloat16)


def packed_rows(shapes):
    return sum(pl.cdiv(cols, 128) * rows for rows, cols in shapes)


def tiles_of(shapes):
    base = 0
    for index, (rows, cols) in enumerate(shapes):
        for start in range(0, cols, 128):
            yield index, base, rows, start, min(128, cols - start)
            base += rows


def piece_rows(shapes, devices):
    return pl.cdiv(pl.cdiv(packed_rows(shapes), devices), 16) * 16


class Exchange:
    def __init__(self, source, held, sems, slabs, ring):
        self.slabs = slabs
        self.source, self.held, self.sems = source, held, sems
        self.vol, self.slab = ring.vol, ring.slab

    def copy(self, step):
        other = lax.rem(self.slab + step, self.slabs)
        return pltpu.make_async_remote_copy(
            src_ref=self.source.at[other],
            dst_ref=self.held.at[self.slab],
            send_sem=self.sems.at[0, step],
            recv_sem=self.sems.at[1, step],
            device_id=(self.vol, other),
            device_id_type=MESH,
        )

    def start(self):
        for step in range(1, self.slabs):
            self.copy(step).start()
        self.held[self.slab] = self.source[self.slab]

    def wait_all(self):
        for step in range(1, self.slabs):
            self.copy(step).wait_recv()

    def drain(self):
        for step in range(1, self.slabs):
            self.copy(step).wait_send()


class Ring:
    def __init__(self, slabs, chips):
        self.slabs, self.chips = slabs, chips
        self.vol = lax.axis_index("vol")
        self.slab = lax.axis_index("slab")
        self.core = lax.rem(self.vol, 2)
        self.me = (self.vol // 2) * slabs + self.slab
        self.pair = (self.vol + 1 - 2 * self.core, self.slab)

    def peer(self, step):
        other = lax.rem(self.me + step, self.chips)
        return ((other // self.slabs) * 2 + self.core, lax.rem(other, self.slabs))

    def steps(self, action, first=1):
        def body(step, carry):
            action(step)
            return carry

        lax.fori_loop(first, self.chips, body, 0)

    def greet(self):
        barrier = pltpu.get_barrier_semaphore()
        pl.semaphore_signal(barrier, inc=1, device_id=self.pair, device_id_type=MESH)
        self.steps(
            lambda step: pl.semaphore_signal(
                barrier, inc=1, device_id=self.peer(step), device_id_type=MESH
            )
        )
        pl.semaphore_wait(barrier, self.chips)


class Summed:
    def __init__(self, ring, own, from_pair, mine, landed, total, whole, pair_sems, sems):
        self.ring = ring
        self.own, self.from_pair, self.mine = own, from_pair, mine
        self.landed, self.total, self.whole = landed, total, whole
        self.pair_sems, self.sems = pair_sems, sems
        self.piece = total.shape[0]
        self.half = ring.chips * self.piece
        self.base = ring.core * ring.chips

    def rows(self, index):
        return pl.ds(pl.multiple_of(index * self.piece, 16), self.piece)

    def halves(self, index):
        return pl.ds(pl.multiple_of(index * self.half, 16), self.half)

    def remote(self, source, target, kind, step, device):
        return pltpu.make_async_remote_copy(
            src_ref=source,
            dst_ref=target,
            send_sem=self.sems.at[kind, 0, step],
            recv_sem=self.sems.at[kind, 1, step],
            device_id=device,
            device_id_type=MESH,
        )

    def swap(self):
        return pltpu.make_async_remote_copy(
            src_ref=self.own.at[self.halves(1 - self.ring.core)],
            dst_ref=self.from_pair,
            send_sem=self.pair_sems.at[0],
            recv_sem=self.pair_sems.at[1],
            device_id=self.ring.pair,
            device_id_type=MESH,
        )

    def outward(self, step):
        other = lax.rem(self.ring.me + step, self.ring.chips)
        source, target = self.mine.at[self.rows(other)], self.landed.at[self.rows(step)]
        return self.remote(source, target, 0, step, self.ring.peer(step))

    def back(self, step):
        target = self.whole.at[self.rows(self.base + self.ring.me)]
        return self.remote(self.total, target, 1, step, self.ring.peer(step))

    def across(self, step):
        chips = self.ring.chips
        block = self.whole.at[self.rows(self.base + lax.rem(self.ring.me - step + chips, chips))]
        return self.remote(block, block, 2, step, self.ring.pair)

    def scatter(self):
        self.swap().wait()
        own = self.own[self.halves(self.ring.core), :].astype(jnp.float32)
        self.mine[...] = half(own + self.from_pair[...].astype(jnp.float32))
        self.ring.steps(lambda step: self.outward(step).start())

    def gather(self):
        def add(step, running):
            self.outward(step).wait_recv()
            return running + self.landed[self.rows(step), :].astype(jnp.float32)

        start = self.mine[self.rows(self.ring.me), :].astype(jnp.float32)
        self.total[...] = half(lax.fori_loop(1, self.ring.chips, add, start))
        self.whole[self.rows(self.base + self.ring.me), :] = self.total[...]
        self.ring.steps(lambda step: self.back(step).start())

    def hand_on(self):
        self.across(0).start()

        def pass_on(step):
            self.back(step).wait_recv()
            self.across(step).start()

        self.ring.steps(pass_on)

    def settle(self):
        self.ring.steps(lambda step: self.across(step).wait(), 0)

        def drain(step):
            self.outward(step).wait_send()
            self.back(step).wait_send()

        self.ring.steps(drain)


def step_kernel(shapes, slabs, chips, volumes, w1, w2, w3, mg, spread, pick1, pick2, pick3, back2,
                back3, taps, order, out, p1, p2, p3, w1b, w2p, w3p, a2, even3, odd3, even2, odd2,
                rows2, g2, vol, vol_sems, *parts):
    ring = Ring(slabs, chips)
    ring.greet()
    incoming = Exchange(volumes, vol, vol_sems, slabs, ring)
    incoming.start()
    late, early = Summed(ring, *parts[:8]), Summed(ring, *parts[8:])
    late.own[...] = jnp.zeros_like(late.own)
    early.own[...] = jnp.zeros_like(early.own)

    f32 = jnp.float32
    channels = vol.shape[1]
    c1, c2 = w1.shape[0], w2.shape[0]
    blocks = spread.shape[2] // 128
    plane1, plane2 = pick1.shape[0] // 9, pick2.shape[0] // 9
    length2 = mg.shape[0] // plane2
    width1 = blocks * BLOCK * c1
    width2 = length2 * c2

    wide = contract(w1[...], taps[...])
    for pair in range(9):
        tile = wide[:, pair * 128 : (pair + 1) * 128]
        for l in range(BLOCK):
            moved = pltpu.roll(tile, 2 * l * channels, 1) if l else tile
            w1b[l * c1 : (l + 1) * c1, pair * 128 : (pair + 1) * 128] = half(moved)
    w2p[...] = jnp.zeros_like(w2p)
    w3p[...] = jnp.zeros_like(w3p)
    for pair in range(9):
        w2p[:, pair * 128 : pair * 128 + 3 * c1] = w2[:, pair * 3 * c1 : (pair + 1) * 3 * c1]
        w3p[pair * 256 : pair * 256 + 3 * c2, :] = w3[pair * 3 * c2 : (pair + 1) * 3 * c2, :]

    incoming.wait_all()
    levels = []
    for part in range(vol.shape[0]):
        placed = contract(vol[part, 0], spread[0])
        for k in range(1, channels):
            placed = placed + contract(vol[part, k], spread[k])
        levels.append(half(placed))
    r1 = half(contract(pick1[...], jnp.concatenate(levels, axis=0)))
    for pair in range(9):
        for block in range(blocks):
            p1[block * plane1 : (block + 1) * plane1, pair * 128 : (pair + 1) * 128] = r1[
                pair * plane1 : (pair + 1) * plane1, block * 128 : (block + 1) * 128
            ]
    pre1 = contract(p1[...], w1b[...], 1)
    act1 = half(pre1 * sigmoid(pre1))
    a1 = jnp.concatenate(
        [act1[block * plane1 : (block + 1) * plane1, :] for block in range(blocks)], axis=1
    )
    r2 = contract(pick2[...], a1)
    r2 = jnp.concatenate([r2, jnp.zeros((9 * plane2, 128), f32)], axis=1)
    sides = (half(pltpu.roll(r2, c1, 1)), half(pltpu.roll(r2, width1 + 128 - c1, 1)))
    for l in range(length2):
        chunk = sides[l % 2][:, (l // 2) * 128 : (l // 2 + 1) * 128]
        for pair in range(9):
            p2[l * plane2 : (l + 1) * plane2, pair * 128 : (pair + 1) * 128] = chunk[
                pair * plane2 : (pair + 1) * plane2, :
            ]
    pre2 = contract(p2[...], w2p[...], 1)
    act2 = pre2 * sigmoid(pre2)
    for l in range(length2):
        a2[:, l * c2 : (l + 1) * c2] = act2[l * plane2 : (l + 1) * plane2, :]
    r3 = contract(pick3[...], half(a2[...]))
    r3 = jnp.concatenate([r3, jnp.zeros((9 * plane2, 256), f32)], axis=1)
    sides = (half(pltpu.roll(r3, c2, 1)), half(r3))
    for l in range(length2):
        chunk = sides[l % 2][:, (l // 2) * 128 : (l // 2) * 128 + 256]
        for pair in range(9):
            p3[l * plane2 : (l + 1) * plane2, pair * 256 : (pair + 1) * 256] = chunk[
                pair * plane2 : (pair + 1) * plane2, :
            ]
    pre3 = contract(p3[...], w3p[...])
    given = contract(order[...], mg[...])
    slope3 = given * slope_of(pre3)
    delta3 = half(slope3)
    grad3 = contract(half(slope3.T), p3[...])
    for pair in range(9):
        for lane in range(0, 3 * c2, 128):
            wide = min(128, 3 * c2 - lane)
            turned = grad3[:, pair * 256 + lane : pair * 256 + lane + 128].T
            at = pair * 3 * c2 + lane
            late.own[at : at + wide, :] = half(turned[:wide, :])
    late.swap().start()

    spread3 = contract(delta3, w3p[...], 1)
    for pair in range(9):
        for side, holder in ((0, even3), (1, odd3)):
            for tile in range(length2 // 2 + 1):
                total = None
                for part in range(2):
                    l = 2 * (tile - part) + side
                    if 0 <= l < length2:
                        piece = spread3[
                            l * plane2 : (l + 1) * plane2,
                            pair * 256 + part * 128 : pair * 256 + part * 128 + 128,
                        ]
                        total = piece if total is None else total + piece
                holder[pair * plane2 : (pair + 1) * plane2, tile * 128 : (tile + 1) * 128] = total
    down = contract_fine(back3[...], even3[...])
    down = pltpu.roll(down, down.shape[1] - c2, 1) + contract_fine(back3[...], odd3[...])
    for l in range(length2):
        rows2[l * plane2 : (l + 1) * plane2, :] = down[:, l * c2 : (l + 1) * c2]
    slope2 = half(rows2[...]).astype(f32) * slope_of(pre2)
    delta2 = half(slope2)
    late.scatter()
    grad2 = contract(half(slope2.T), p2[...])
    g2[...] = jnp.zeros_like(g2)
    for pair in range(9):
        g2[:, pair * 3 * c1 : (pair + 1) * 3 * c1] = grad2[:, pair * 128 : pair * 128 + 3 * c1]

    spread2 = contract(delta2, w2p[...])
    for pair in range(9):
        for l in range(length2):
            holder = odd2 if l % 2 else even2
            holder[pair * plane2 : (pair + 1) * plane2, (l // 2) * 128 : (l // 2 + 1) * 128] = spread2[
                l * plane2 : (l + 1) * plane2, pair * 128 : (pair + 1) * 128
            ]
    tail = jnp.zeros((plane1, 128), f32)
    left = jnp.concatenate([contract_fine(back2[...], even2[...]), tail], axis=1)
    right = jnp.concatenate([contract_fine(back2[...], odd2[...]), tail], axis=1)
    down = pltpu.roll(left, width1 + 128 - c1, 1) + pltpu.roll(right, c1, 1)
    step = BLOCK * c1
    down = jnp.concatenate([down[:, block * step : (block + 1) * step] for block in range(blocks)], axis=0)
    slope1 = down * slope_of(pre1)
    grad1 = contract(half(slope1.T), p1[...])
    tiles = []
    for pair in range(9):
        total = grad1[:c1, pair * 128 : (pair + 1) * 128]
        for l in range(1, BLOCK):
            tile = grad1[l * c1 : (l + 1) * c1, pair * 128 : (pair + 1) * 128]
            total = total + pltpu.roll(tile, 128 - 2 * l * channels, 1)
        tiles.append(half(total))
    first = contract(jnp.concatenate(tiles, axis=1), taps[...], 1)

    for index, base, rows, start, width in tiles_of(shapes[:2]):
        if index == 0:
            early.own[base : base + rows, :width] = half(first)
        else:
            early.own[base : base + rows, :] = half(g2[:, start : start + 128])
    early.swap().start()
    late.gather()
    early.scatter()
    late.hand_on()
    early.gather()
    early.hand_on()
    late.settle()
    early.settle()
    incoming.drain()
    out[: late.whole.shape[0], :] = late.whole[...]
    out[late.whole.shape[0] :, :] = early.whole[...]


def unpack_kernel(shapes, bases, factor, packed, first, second, third):
    for out, shape, base in ((first, shapes[:1], bases[0]), (second, shapes[1:2], bases[1])):
        for index, at, rows, start, width in tiles_of(shape):
            tile = packed[base + at : base + at + rows, :].astype(jnp.float32) * factor
            out[:, start : start + width] = tile[:, :width]
    third[...] = packed[: third.shape[0], :].astype(jnp.float32) * factor


def per_device(volumes, w_first, w_second, w_third, map_grad):
    slabs = lax.axis_size("slab")
    devices = lax.axis_size("vol") * slabs
    chips = devices // 2
    factor = 1.0 / (map_grad.shape[0] * devices)
    shapes = (w_first.shape, w_second.shape, w_third.shape)
    parts, channels, level, height, width = volumes.shape
    depth = level * slabs
    tables = tables_of(channels, depth, height, width)
    c1, c2, c3 = w_first.shape[0], w_second.shape[0], w_third.shape[0]
    plane1 = depth * height // 4
    plane2 = depth * height // 16
    length2 = width // 4
    cells = plane2 * length2
    bf16, f32 = jnp.bfloat16, jnp.float32
    late_piece = piece_rows(((27 * c2, c3),), devices)
    early_piece = piece_rows(shapes[:2], devices)
    scratch = [
        ((width // (2 * BLOCK) * plane1, 9 * 128), bf16),
        ((cells, 9 * 128), bf16),
        ((cells, 9 * 256), bf16),
        ((BLOCK * c1, 9 * 128), bf16),
        ((c2, 9 * 128), bf16),
        ((9 * 256, c3), bf16),
        ((plane2, length2 * c2), f32),
        ((9 * plane2, length2 * c2 + 128), f32),
        ((9 * plane2, length2 * c2 + 128), f32),
        ((9 * plane2, width // 2 * c1), f32),
        ((9 * plane2, width // 2 * c1), f32),
        ((cells, c2), f32),
        ((c2, pl.cdiv(27 * c1, 128) * 128), f32),
        ((slabs, channels, level * height, width), bf16),
    ]
    scratch = [pltpu.VMEM(shape, kind) for shape, kind in scratch]
    dma = pltpu.SemaphoreType.DMA
    scratch.append(dma((2, slabs)))
    for piece in (late_piece, early_piece):
        for count in (devices, chips, chips, chips, 1, devices):
            scratch.append(pltpu.VMEM((count * piece, 128), bf16))
        scratch += [dma((2,)), dma((3, 2, chips))]
    operands = (
        volumes.reshape(parts, channels, level * height, width),
        w_first,
        w_second,
        w_third.T,
        map_grad[0].transpose(1, 2, 3, 0).reshape(cells, c3),
        *tables,
    )
    in_vmem = pl.BlockSpec(memory_space=pltpu.VMEM)
    packed = pl.pallas_call(
        functools.partial(step_kernel, shapes, slabs, chips),
        out_shape=jax.ShapeDtypeStruct((devices * (late_piece + early_piece), 128), bf16),
        in_specs=[in_vmem] * len(operands),
        out_specs=in_vmem,
        scratch_shapes=scratch,
        compiler_params=pltpu.CompilerParams(
            collective_id=0, has_side_effects=True, vmem_limit_bytes=56 << 20
        ),
        name="step",
    )(*operands)
    early_base = devices * late_piece
    bases = (early_base, early_base + packed_rows(shapes[:1]))
    outs = (shapes[0], shapes[1], (27 * c2, c3))
    first, second, third = pl.pallas_call(
        functools.partial(unpack_kernel, shapes, bases, factor),
        out_shape=[jax.ShapeDtypeStruct(shape, f32) for shape in outs],
        in_specs=[in_vmem],
        out_specs=[in_vmem] * 3,
        name="unpack",
    )(packed)
    return first, second, third.T


def solution(mesh):
    return jax.shard_map(
        per_device,
        mesh=mesh,
        in_specs=(
            P("vol", None, "slab", None, None),
            P(),
            P(),
            P(),
            P(("vol", "slab"), None, None, None, None),
        ),
        out_specs=(P(), P(), P()),
        check_vma=False,
    )
```

time: 51.4 us -> 45.4 us (0.88)
  the two profiles are of different devices: /device:TPU:25 before, /device:TPU:0 now
where the time goes in v1:
time: 45.4 us; the launch traced here: 45.2 us
  Pallas kernels  44.6 us (98%)
  between operations  0.64 us (1%)
    pallas_call x1, Pallas kernels, per_device(): pl.pallas_call(functools.partial(step_kernel, shapes, slabs, chips), out_...  42.5 us
    pallas_call x1, Pallas kernels, per_device(): pl.pallas_call(functools.partial(unpack_kernel, shapes, bases, factor), o...  2.1 us

profile of v1, /device:TPU:0, one launch (start us, length us, event | category | flops | bytes accessed | tf_op | source)
XLA Modules:
  0.0 45.2 jit_solution(368873063511045223)
XLA Ops:
  0.6 42.5 %step.1.packed = bf16[2560,128]{1,0:T(8,128)(2,1)} custom-call(bf16[2,4,128,64]{3,2,1,0:T(8,128)(2,1)} %bitcast.9, bf16[32,108]{1,0:T(8,128)(2,1)} %w1.1, bf16[64,864]{1,0:T(8,128)(2,1)} %w2.1, bf16[1728,128]{1,0:T(8,128)(2,1)} %bitcast.8, bf16[256,128]{1,0:T(8,128)(2,1)} %bitcast.10, bf16[4,64,512]{2,1,0:T(8,128)(2,1)} %constant.16.clone.spread, ...), custom_call_target="tpu_custom_call" | custom-call | tf_op jit(solution)/shard_map/step/pallas_call | solution.py:463
  43.1 2.1 %unpack.1 = (f32[32,108]{1,0:T(8,128)}, f32[64,864]{1,0:T(8,128)}, f32[1728,128]{1,0:T(8,128)}) custom-call(bf16[2560,128]{1,0:T(8,128)(2,1)} %step.1.packed), custom_call_target="tpu_custom_call" | custom-call | tf_op jit(solution)/shard_map/unpack/pallas_call | solution.py:477

commit v2 on v1

--- a/solution.py
+++ b/solution.py
@@ -135,58 +135,62 @@
 
 
 class Ring:
-    def __init__(self, slabs, chips):
-        self.slabs, self.chips = slabs, chips
+    def __init__(self, slabs, lines):
+        self.slabs, self.lines, self.planes = slabs, lines, 2 * slabs
         self.vol = lax.axis_index("vol")
         self.slab = lax.axis_index("slab")
         self.core = lax.rem(self.vol, 2)
-        self.me = (self.vol // 2) * slabs + self.slab
+        self.side = lax.rem(self.vol // 2, 2)
+        self.at_line = self.vol // 4
+        self.at_plane = self.side * slabs + self.slab
         self.pair = (self.vol + 1 - 2 * self.core, self.slab)
 
-    def peer(self, step):
-        other = lax.rem(self.me + step, self.chips)
-        return ((other // self.slabs) * 2 + self.core, lax.rem(other, self.slabs))
-
-    def steps(self, action, first=1):
-        def body(step, carry):
-            action(step)
-            return carry
-
-        lax.fori_loop(first, self.chips, body, 0)
+    def in_plane(self, step):
+        other = lax.rem(self.at_plane + step, self.planes)
+        vol = (self.at_line * 2 + other // self.slabs) * 2 + self.core
+        return other, (vol, lax.rem(other, self.slabs))
+
+    def in_line(self, step):
+        other = lax.rem(self.at_line + step, self.lines)
+        return other, ((other * 2 + self.side) * 2 + self.core, self.slab)
 
     def greet(self):
         barrier = pltpu.get_barrier_semaphore()
-        pl.semaphore_signal(barrier, inc=1, device_id=self.pair, device_id_type=MESH)
-        self.steps(
-            lambda step: pl.semaphore_signal(
-                barrier, inc=1, device_id=self.peer(step), device_id_type=MESH
-            )
-        )
-        pl.semaphore_wait(barrier, self.chips)
+        partners = [self.pair]
+        partners += [self.in_plane(step)[1] for step in range(1, self.planes)]
+        partners += [self.in_line(step)[1] for step in range(1, self.lines)]
+        for partner in partners:
+            pl.semaphore_signal(barrier, inc=1, device_id=partner, device_id_type=MESH)
+        pl.semaphore_wait(barrier, len(partners))
 
 
 class Summed:
-    def __init__(self, ring, own, from_pair, mine, landed, total, whole, pair_sems, sems):
+    def __init__(self, ring, own, from_pair, mine, landed, middle, lined, total, whole, *sems):
         self.ring = ring
         self.own, self.from_pair, self.mine = own, from_pair, mine
-        self.landed, self.total, self.whole = landed, total, whole
-        self.pair_sems, self.sems = pair_sems, sems
+        self.landed, self.middle, self.lined = landed, middle, lined
+        self.total, self.whole = total, whole
+        self.pair_sems, self.plane_sems, self.line_sems = sems
         self.piece = total.shape[0]
-        self.half = ring.chips * self.piece
-        self.base = ring.core * ring.chips
-
-    def rows(self, index):
+        self.block = ring.lines * self.piece
+        self.half = ring.planes * self.block
+        self.spot = ring.core * ring.planes + ring.at_plane
+
+    def pieces(self, index):
         return pl.ds(pl.multiple_of(index * self.piece, 16), self.piece)
+
+    def blocks(self, index):
+        return pl.ds(pl.multiple_of(index * self.block, 16), self.block)
 
     def halves(self, index):
         return pl.ds(pl.multiple_of(index * self.half, 16), self.half)
 
-    def remote(self, source, target, kind, step, device):
+    def remote(self, source, target, sems, kind, step, device):
         return pltpu.make_async_remote_copy(
             src_ref=source,
             dst_ref=target,
-            send_sem=self.sems.at[kind, 0, step],
-            recv_sem=self.sems.at[kind, 1, step],
+            send_sem=sems.at[kind, 0, step],
+            recv_sem=sems.at[kind, 1, step],
             device_id=device,
             device_id_type=MESH,
         )
@@ -201,63 +205,88 @@
             device_id_type=MESH,
         )
 
-    def outward(self, step):
-        other = lax.rem(self.ring.me + step, self.ring.chips)
-        source, target = self.mine.at[self.rows(other)], self.landed.at[self.rows(step)]
-        return self.remote(source, target, 0, step, self.ring.peer(step))
-
-    def back(self, step):
-        target = self.whole.at[self.rows(self.base + self.ring.me)]
-        return self.remote(self.total, target, 1, step, self.ring.peer(step))
+    def plane_out(self, step):
+        other, device = self.ring.in_plane(step)
+        source, target = self.mine.at[self.blocks(other)], self.landed.at[self.blocks(step)]
+        return self.remote(source, target, self.plane_sems, 0, step, device)
+
+    def line_out(self, step):
+        other, device = self.ring.in_line(step)
+        source, target = self.middle.at[self.pieces(other)], self.lined.at[self.pieces(step)]
+        return self.remote(source, target, self.line_sems, 0, step, device)
+
+    def line_back(self, step):
+        lines = self.ring.lines
+        target = self.whole.at[self.pieces(self.spot * lines + self.ring.at_line)]
+        return self.remote(self.total, target, self.line_sems, 1, step, self.ring.in_line(step)[1])
+
+    def plane_back(self, step):
+        block = self.whole.at[self.blocks(self.spot)]
+        return self.remote(block, block, self.plane_sems, 1, step, self.ring.in_plane(step)[1])
 
     def across(self, step):
-        chips = self.ring.chips
-        block = self.whole.at[self.rows(self.base + lax.rem(self.ring.me - step + chips, chips))]
-        return self.remote(block, block, 2, step, self.ring.pair)
+        planes = self.ring.planes
+        source = lax.rem(self.ring.at_plane - step + planes, planes)
+        block = self.whole.at[self.blocks(self.ring.core * planes + source)]
+        return self.remote(block, block, self.plane_sems, 2, step, self.ring.pair)
 
     def scatter(self):
         self.swap().wait()
         own = self.own[self.halves(self.ring.core), :].astype(jnp.float32)
         self.mine[...] = half(own + self.from_pair[...].astype(jnp.float32))
-        self.ring.steps(lambda step: self.outward(step).start())
-
-    def gather(self):
-        def add(step, running):
-            self.outward(step).wait_recv()
-            return running + self.landed[self.rows(step), :].astype(jnp.float32)
-
-        start = self.mine[self.rows(self.ring.me), :].astype(jnp.float32)
-        self.total[...] = half(lax.fori_loop(1, self.ring.chips, add, start))
-        self.whole[self.rows(self.base + self.ring.me), :] = self.total[...]
-        self.ring.steps(lambda step: self.back(step).start())
-
-    def hand_on(self):
+        for step in range(1, self.ring.planes):
+            self.plane_out(step).start()
+
+    def gather_plane(self):
+        running = self.mine[self.blocks(self.ring.at_plane), :].astype(jnp.float32)
+        for step in range(1, self.ring.planes):
+            self.plane_out(step).wait_recv()
+            running = running + self.landed[self.blocks(step), :].astype(jnp.float32)
+        self.middle[...] = half(running)
+        for step in range(1, self.ring.lines):
+            self.line_out(step).start()
+
+    def gather_line(self):
+        running = self.middle[self.pieces(self.ring.at_line), :].astype(jnp.float32)
+        for step in range(1, self.ring.lines):
+            self.line_out(step).wait_recv()
+            running = running + self.lined[self.pieces(step), :].astype(jnp.float32)
+        self.total[...] = half(running)
+        for step in range(1, self.ring.lines):
+            self.line_back(step).start()
+        self.whole[self.pieces(self.spot * self.ring.lines + self.ring.at_line), :] = self.total[...]
+
+    def spread(self):
+        for step in range(1, self.ring.lines):
+            self.line_back(step).wait_recv()
+        for step in range(1, self.ring.planes):
+            self.plane_back(step).start()
         self.across(0).start()
 
-        def pass_on(step):
-            self.back(step).wait_recv()
+    def pass_on(self):
+        for step in range(1, self.ring.planes):
+            self.plane_back(step).wait_recv()
             self.across(step).start()
 
-        self.ring.steps(pass_on)
-
     def settle(self):
-        self.ring.steps(lambda step: self.across(step).wait(), 0)
-
-        def drain(step):
-            self.outward(step).wait_send()
-            self.back(step).wait_send()
-
-        self.ring.steps(drain)
-
-
-def step_kernel(shapes, slabs, chips, volumes, w1, w2, w3, mg, spread, pick1, pick2, pick3, back2,
+        for step in range(self.ring.planes):
+            self.across(step).wait()
+        for step in range(1, self.ring.planes):
+            self.plane_out(step).wait_send()
+            self.plane_back(step).wait_send()
+        for step in range(1, self.ring.lines):
+            self.line_out(step).wait_send()
+            self.line_back(step).wait_send()
+
+
+def step_kernel(shapes, slabs, lines, volumes, w1, w2, w3, mg, spread, pick1, pick2, pick3, back2,
                 back3, taps, order, out, p1, p2, p3, w1b, w2p, w3p, a2, even3, odd3, even2, odd2,
                 rows2, g2, vol, vol_sems, *parts):
-    ring = Ring(slabs, chips)
+    ring = Ring(slabs, lines)
     ring.greet()
     incoming = Exchange(volumes, vol, vol_sems, slabs, ring)
     incoming.start()
-    late, early = Summed(ring, *parts[:8]), Summed(ring, *parts[8:])
+    late, early = Summed(ring, *parts[:11]), Summed(ring, *parts[11:])
     late.own[...] = jnp.zeros_like(late.own)
     early.own[...] = jnp.zeros_like(early.own)
 
@@ -368,6 +397,7 @@
             holder[pair * plane2 : (pair + 1) * plane2, (l // 2) * 128 : (l // 2 + 1) * 128] = spread2[
                 l * plane2 : (l + 1) * plane2, pair * 128 : (pair + 1) * 128
             ]
+    late.gather_plane()
     tail = jnp.zeros((plane1, 128), f32)
     left = jnp.concatenate([contract_fine(back2[...], even2[...]), tail], axis=1)
     right = jnp.concatenate([contract_fine(back2[...], odd2[...]), tail], axis=1)
@@ -391,11 +421,14 @@
         else:
             early.own[base : base + rows, :] = half(g2[:, start : start + 128])
     early.swap().start()
-    late.gather()
+    late.gather_line()
     early.scatter()
-    late.hand_on()
-    early.gather()
-    early.hand_on()
+    late.spread()
+    early.gather_plane()
+    late.pass_on()
+    early.gather_line()
+    early.spread()
+    early.pass_on()
     late.settle()
     early.settle()
     incoming.drain()
@@ -415,6 +448,7 @@
     slabs = lax.axis_size("slab")
     devices = lax.axis_size("vol") * slabs
     chips = devices // 2
+    lines = chips // (2 * slabs)
     factor = 1.0 / (map_grad.shape[0] * devices)
     shapes = (w_first.shape, w_second.shape, w_third.shape)
     parts, channels, level, height, width = volumes.shape
@@ -448,9 +482,9 @@
     dma = pltpu.SemaphoreType.DMA
     scratch.append(dma((2, slabs)))
     for piece in (late_piece, early_piece):
-        for count in (devices, chips, chips, chips, 1, devices):
+        for count in (devices, chips, chips, chips, lines, lines, 1, devices):
             scratch.append(pltpu.VMEM((count * piece, 128), bf16))
-        scratch += [dma((2,)), dma((3, 2, chips))]
+        scratch += [dma((2,)), dma((3, 2, 2 * slabs)), dma((2, 2, lines))]
     operands = (
         volumes.reshape(parts, channels, level * height, width),
         w_first,
@@ -461,7 +495,7 @@
     )
     in_vmem = pl.BlockSpec(memory_space=pltpu.VMEM)
     packed = pl.pallas_call(
-        functools.partial(step_kernel, shapes, slabs, chips),
+        functools.partial(step_kernel, shapes, slabs, lines),
         out_shape=jax.ShapeDtypeStruct((devices * (late_piece + early_piece), 128), bf16),
         in_specs=[in_vmem] * len(operands),
         out_specs=in_vmem,

time: 45.4 us -> 44.8 us (0.987)
  Pallas kernels: 44.6 us -> 44 us
    pallas_call x1, Pallas kernels: 42.5 us -> 41.9 us  [per_device(): pl.pallas_call(functools.partial(step_kernel, shapes, slabs, lines), out_...]
where the time goes in v2:
time: 44.8 us; the launch traced here: 44.7 us
  Pallas kernels  44 us (98%)
  between operations  0.64 us (1%)
    pallas_call x1, Pallas kernels, per_device(): pl.pallas_call(functools.partial(step_kernel, shapes, slabs, lines), out_...  41.9 us
    pallas_call x1, Pallas kernels, per_device(): pl.pallas_call(functools.partial(unpack_kernel, shapes, bases, factor), o...  2.1 us

profile of v2, /device:TPU:0, one launch (start us, length us, event | category | flops | bytes accessed | tf_op | source)
XLA Modules:
  0.0 44.7 jit_solution(3687170776601699847)
XLA Ops:
  0.6 41.9 %step.1.packed = bf16[2560,128]{1,0:T(8,128)(2,1)} custom-call(bf16[2,4,128,64]{3,2,1,0:T(8,128)(2,1)} %bitcast.9, bf16[32,108]{1,0:T(8,128)(2,1)} %w1.1, bf16[64,864]{1,0:T(8,128)(2,1)} %w2.1, bf16[1728,128]{1,0:T(8,128)(2,1)} %bitcast.8, bf16[256,128]{1,0:T(8,128)(2,1)} %bitcast.10, bf16[4,64,512]{2,1,0:T(8,128)(2,1)} %constant.16.clone.spread, ...), custom_call_target="tpu_custom_call" | custom-call | tf_op jit(solution)/shard_map/step/pallas_call | solution.py:497
  42.6 2.1 %unpack.1 = (f32[32,108]{1,0:T(8,128)}, f32[64,864]{1,0:T(8,128)}, f32[1728,128]{1,0:T(8,128)}) custom-call(bf16[2560,128]{1,0:T(8,128)(2,1)} %step.1.packed), custom_call_target="tpu_custom_call" | custom-call | tf_op jit(solution)/shard_map/unpack/pallas_call | solution.py:511

commit v3 on v2

--- a/solution.py
+++ b/solution.py
@@ -165,19 +165,15 @@
 
 
 class Summed:
-    def __init__(self, ring, own, from_pair, mine, landed, middle, lined, total, whole, *sems):
+    def __init__(self, ring, own, from_pair, mine, landed, middle, lined, whole, *sems):
         self.ring = ring
         self.own, self.from_pair, self.mine = own, from_pair, mine
         self.landed, self.middle, self.lined = landed, middle, lined
-        self.total, self.whole = total, whole
+        self.whole = whole
         self.pair_sems, self.plane_sems, self.line_sems = sems
-        self.piece = total.shape[0]
-        self.block = ring.lines * self.piece
+        self.block = middle.shape[0]
         self.half = ring.planes * self.block
         self.spot = ring.core * ring.planes + ring.at_plane
-
-    def pieces(self, index):
-        return pl.ds(pl.multiple_of(index * self.piece, 16), self.piece)
 
     def blocks(self, index):
         return pl.ds(pl.multiple_of(index * self.block, 16), self.block)
@@ -211,14 +207,8 @@
         return self.remote(source, target, self.plane_sems, 0, step, device)
 
     def line_out(self, step):
-        other, device = self.ring.in_line(step)
-        source, target = self.middle.at[self.pieces(other)], self.lined.at[self.pieces(step)]
-        return self.remote(source, target, self.line_sems, 0, step, device)
-
-    def line_back(self, step):
-        lines = self.ring.lines
-        target = self.whole.at[self.pieces(self.spot * lines + self.ring.at_line)]
-        return self.remote(self.total, target, self.line_sems, 1, step, self.ring.in_line(step)[1])
+        target = self.lined.at[self.blocks(self.ring.at_line)]
+        return self.remote(self.middle, target, self.line_sems, 0, step, self.ring.in_line(step)[1])
 
     def plane_back(self, step):
         block = self.whole.at[self.blocks(self.spot)]
@@ -247,18 +237,15 @@
             self.line_out(step).start()
 
     def gather_line(self):
-        running = self.middle[self.pieces(self.ring.at_line), :].astype(jnp.float32)
+        self.lined[self.blocks(self.ring.at_line), :] = self.middle[...]
         for step in range(1, self.ring.lines):
             self.line_out(step).wait_recv()
-            running = running + self.lined[self.pieces(step), :].astype(jnp.float32)
-        self.total[...] = half(running)
-        for step in range(1, self.ring.lines):
-            self.line_back(step).start()
-        self.whole[self.pieces(self.spot * self.ring.lines + self.ring.at_line), :] = self.total[...]
+        running = self.lined[: self.block, :].astype(jnp.float32)
+        for index in range(1, self.ring.lines):
+            running = running + self.lined[self.blocks(index), :].astype(jnp.float32)
+        self.whole[self.blocks(self.spot), :] = half(running)
 
     def spread(self):
-        for step in range(1, self.ring.lines):
-            self.line_back(step).wait_recv()
         for step in range(1, self.ring.planes):
             self.plane_back(step).start()
         self.across(0).start()
@@ -276,7 +263,6 @@
             self.plane_back(step).wait_send()
         for step in range(1, self.ring.lines):
             self.line_out(step).wait_send()
-            self.line_back(step).wait_send()
 
 
 def step_kernel(shapes, slabs, lines, volumes, w1, w2, w3, mg, spread, pick1, pick2, pick3, back2,
@@ -286,7 +272,7 @@
     ring.greet()
     incoming = Exchange(volumes, vol, vol_sems, slabs, ring)
     incoming.start()
-    late, early = Summed(ring, *parts[:11]), Summed(ring, *parts[11:])
+    late, early = Summed(ring, *parts[:10]), Summed(ring, *parts[10:])
     late.own[...] = jnp.zeros_like(late.own)
     early.own[...] = jnp.zeros_like(early.own)
 
@@ -482,9 +468,9 @@
     dma = pltpu.SemaphoreType.DMA
     scratch.append(dma((2, slabs)))
     for piece in (late_piece, early_piece):
-        for count in (devices, chips, chips, chips, lines, lines, 1, devices):
+        for count in (devices, chips, chips, chips, lines, lines * lines, devices):
             scratch.append(pltpu.VMEM((count * piece, 128), bf16))
-        scratch += [dma((2,)), dma((3, 2, 2 * slabs)), dma((2, 2, lines))]
+        scratch += [dma((2,)), dma((3, 2, 2 * slabs)), dma((1, 2, lines))]
     operands = (
         volumes.reshape(parts, channels, level * height, width),
         w_first,

time: 44.8 us -> 43.9 us (0.980)
  Pallas kernels: 44 us -> 43.1 us
    pallas_call x1, Pallas kernels: 41.9 us -> 41 us  [per_device(): pl.pallas_call(functools.partial(step_kernel, shapes, slabs, lines), out_...]
where the time goes in v3:
time: 43.9 us; the launch traced here: 43.7 us
  Pallas kernels  43.1 us (98%)
  between operations  0.64 us (1%)
    pallas_call x1, Pallas kernels, per_device(): pl.pallas_call(functools.partial(step_kernel, shapes, slabs, lines), out_...  41 us
    pallas_call x1, Pallas kernels, per_device(): pl.pallas_call(functools.partial(unpack_kernel, shapes, bases, factor), o...  2.1 us

profile of v3, /device:TPU:0, one launch (start us, length us, event | category | flops | bytes accessed | tf_op | source)
XLA Modules:
  0.0 43.7 jit_solution(11555797514829618412)
XLA Ops:
  0.6 41.0 %step.1.packed = bf16[2560,128]{1,0:T(8,128)(2,1)} custom-call(bf16[2,4,128,64]{3,2,1,0:T(8,128)(2,1)} %bitcast.9, bf16[32,108]{1,0:T(8,128)(2,1)} %w1.1, bf16[64,864]{1,0:T(8,128)(2,1)} %w2.1, bf16[1728,128]{1,0:T(8,128)(2,1)} %bitcast.8, bf16[256,128]{1,0:T(8,128)(2,1)} %bitcast.10, bf16[4,64,512]{2,1,0:T(8,128)(2,1)} %constant.16.clone.spread, ...), custom_call_target="tpu_custom_call" | custom-call | tf_op jit(solution)/shard_map/step/pallas_call | solution.py:483
  41.6 2.1 %unpack.1 = (f32[32,108]{1,0:T(8,128)}, f32[64,864]{1,0:T(8,128)}, f32[1728,128]{1,0:T(8,128)}) custom-call(bf16[2560,128]{1,0:T(8,128)(2,1)} %step.1.packed), custom_call_target="tpu_custom_call" | custom-call | tf_op jit(solution)/shard_map/unpack/pallas_call | solution.py:497
